TPU v7x, 32 devices: a whole 2x2x4 slice. The times are simulated.
32 devices in a mesh: fsdp: 4 (over z), tensor: 8 (over y, x, core).
Axes of the slice: x: 2, y: 2, z: 4, core: 2. Of those that a mesh axis runs over, the one named last changes fastest.
Arguments:
- tokens: bfloat16 [5120, 2048], P(('fsdp', 'tensor')), may hold values from -6 to 6
- gain_attn: bfloat16 [2048], replicated, may hold values from 0.099609375 to 1.8984375
- gain_mlp: bfloat16 [2048], replicated, may hold values from 0.099609375 to 1.8984375
- w_query: bfloat16 [2048, 2048], P('fsdp', 'tensor'), may hold values from -0.125 to 0.125
- w_key: bfloat16 [2048, 2048], P('fsdp', 'tensor'), may hold values from -0.125 to 0.125
- w_value: bfloat16 [2048, 2048], P('fsdp', 'tensor'), may hold values from -0.125 to 0.125
- w_out: bfloat16 [2048, 2048], P('tensor', 'fsdp'), may hold values from -0.5 to 0.5
- w_gate: bfloat16 [2048, 8192], P('fsdp', 'tensor'), may hold values from -0.125 to 0.125
- w_up: bfloat16 [2048, 8192], P('fsdp', 'tensor'), may hold values from -0.125 to 0.125
- w_down: bfloat16 [8192, 2048], P('tensor', 'fsdp'), may hold values from -0.09375 to 0.09375
- segment_ids: int32 [4, 1280], P('fsdp'), may hold values from 0 to 3, never falling along the last dimension, each value on 1 to 512 neighbouring positions
- out_grad: bfloat16 [5120, 2048], P(('fsdp', 'tensor')), may hold values from -6 to 6
Outputs:
- output: bfloat16 [5120, 2048], P(('fsdp', 'tensor'))
- tokens_grad: bfloat16 [5120, 2048], P(('fsdp', 'tensor'))
- gain_attn_grad: float32 [2048], replicated
- gain_mlp_grad: float32 [2048], replicated
- w_query_grad: float32 [2048, 2048], P('fsdp', 'tensor')
- w_key_grad: float32 [2048, 2048], P('fsdp', 'tensor')
- w_value_grad: float32 [2048, 2048], P('fsdp', 'tensor')
- w_out_grad: float32 [2048, 2048], P('tensor', 'fsdp')
- w_gate_grad: float32 [2048, 8192], P('fsdp', 'tensor')
- w_up_grad: float32 [2048, 8192], P('fsdp', 'tensor')
- w_down_grad: float32 [8192, 2048], P('tensor', 'fsdp')
Inputs may be any that keep to these rules, and one draw needn't show every extreme that they name: `segment_ids`: in each packed row the ids never fall; each sample has 1 to 512 tokens, and some sample in each row has exactly 512.
All inputs are finite; a program needn't handle non-finite values.
Results may differ from a plain program's by a relative error of at most 0.019.
Values may be sent and summed in bfloat16 or wider, within the bound.
A program may use at most 192 MiB of HBM per device.

v0:
```python
import math
import jax
import jax.numpy as jnp
from jax import lax
from jax.sharding import PartitionSpec as P

HEAD = 64
eps = 1e-05
rope_base = 130000.0


def dot_nt(left, right):
    return lax.dot_general(
        left, right, (((1,), (1,)), ((), ())), preferred_element_type=jnp.float32
    )


def dot_tn(left, right):
    return lax.dot_general(
        left, right, (((0,), (0,)), ((), ())), preferred_element_type=jnp.float32
    )


def rope_tables(segments):
    length = segments.shape[1]
    index = jnp.arange(length, dtype=jnp.int32)[None, :]
    change = jnp.concatenate(
        [jnp.ones((segments.shape[0], 1), dtype=bool), segments[:, 1:] != segments[:, :-1]], axis=1
    )
    start = lax.cummax(jnp.where(change, index, 0), axis=1)
    position = (index - start).astype(jnp.float32)
    half = jnp.arange(HEAD // 2, dtype=jnp.float32)
    inverse = jnp.exp(half * (-2.0 / HEAD) * math.log(rope_base))
    angle = position[:, :, None, None] * inverse[None, None, None, :]
    return (jnp.cos(angle), jnp.sin(angle))


def rotate(value, cosine, sine):
    half = value.shape[-1] // 2
    first = value[..., :half]
    second = value[..., half:]
    return jnp.concatenate(
        [first * cosine - second * sine, second * cosine + first * sine], axis=-1
    )


def norm_forward(value, gain):
    scale = lax.rsqrt(jnp.mean(value * value, axis=-1, keepdims=True) + eps)
    return (value * scale * gain, scale)


def norm_backward(value, scale, gain, grad):
    scaled_grad = grad * gain
    inner = jnp.mean(value * scaled_grad, axis=-1, keepdims=True)
    back = scale * scaled_grad - value * scale * scale * scale * inner
    gain_grad = jnp.sum(grad * value * scale, axis=0)
    return (back, gain_grad)


def row_mask(segments):
    length = segments.shape[0]
    index = jnp.arange(length, dtype=jnp.int32)
    return (segments[:, None] == segments[None, :]) & (index[None, :] <= index[:, None])


def row_scores(query, key, segments):
    scores = jnp.einsum("qhd,khd->hqk", query, key, preferred_element_type=jnp.float32) * HEAD ** (
        -0.5
    )
    return jnp.where(row_mask(segments)[None, :, :], scores, -1000000000.0)


def attend_row(inputs):
    query, key, value, segments = inputs
    scores = row_scores(query, key, segments)
    top = jnp.max(scores, axis=-1, keepdims=True)
    expo = jnp.exp(scores - top)
    total = jnp.sum(expo, axis=-1, keepdims=True)
    weights = (expo / total).astype(jnp.bfloat16)
    attended = jnp.einsum("hqk,khd->qhd", weights, value, preferred_element_type=jnp.float32)
    return (attended, (top + jnp.log(total))[..., 0])


def attend_back(inputs):
    query, key, value, segments, logsum, grad_out = inputs
    scores = row_scores(query, key, segments)
    weights = jnp.exp(scores - logsum[..., None])
    grad_value = jnp.einsum(
        "hqk,qhd->khd", weights.astype(jnp.bfloat16), grad_out, preferred_element_type=jnp.float32
    )
    grad_weights = jnp.einsum("qhd,khd->hqk", grad_out, value, preferred_element_type=jnp.float32)
    inner = jnp.sum(weights * grad_weights, axis=-1, keepdims=True)
    grad_scores = (weights * (grad_weights - inner)).astype(jnp.bfloat16)
    grad_query = jnp.einsum(
        "hqk,khd->qhd", grad_scores, key, preferred_element_type=jnp.float32
    ) * HEAD ** (-0.5)
    grad_key = jnp.einsum(
        "hqk,qhd->khd", grad_scores, query, preferred_element_type=jnp.float32
    ) * HEAD ** (-0.5)
    return (grad_query, grad_key, grad_value)


def shards(
    tokens,
    gain_attn,
    gain_mlp,
    w_query,
    w_key,
    w_value,
    w_out,
    w_gate,
    w_up,
    w_down,
    segment_ids,
    out_grad,
):
    rows_grp = segment_ids.shape[0]
    row_len = segment_ids.shape[1]
    local = (w_query, w_key, w_value, w_out, w_gate, w_up, w_down)
    gathered = (
        lax.all_gather(local[0], "fsdp", axis=0, tiled=True),
        lax.all_gather(local[1], "fsdp", axis=0, tiled=True),
        lax.all_gather(local[2], "fsdp", axis=0, tiled=True),
        lax.all_gather(local[3], "fsdp", axis=1, tiled=True),
        lax.all_gather(local[4], "fsdp", axis=0, tiled=True),
        lax.all_gather(local[5], "fsdp", axis=0, tiled=True),
        lax.all_gather(local[6], "fsdp", axis=1, tiled=True),
    )
    wq, wk, wv, wo, wg, wu, wd = gathered
    heads_dev = wq.shape[1] // HEAD
    group = rows_grp * row_len
    gain_a = gain_attn.astype(jnp.float32)
    gain_m = gain_mlp.astype(jnp.float32)
    cosine, sine = rope_tables(segment_ids)

    def heads(value):
        return value.reshape(rows_grp, row_len, heads_dev, HEAD)

    x = tokens.astype(jnp.float32)
    normed_local, scale_a = norm_forward(x, gain_a)
    normed_a = lax.all_gather(normed_local.astype(jnp.bfloat16), "tensor", axis=0, tiled=True)
    query = rotate(
        heads(jnp.dot(normed_a, wq, preferred_element_type=jnp.float32)), cosine, sine
    ).astype(jnp.bfloat16)
    key = rotate(
        heads(jnp.dot(normed_a, wk, preferred_element_type=jnp.float32)), cosine, sine
    ).astype(jnp.bfloat16)
    value = heads(jnp.dot(normed_a, wv, preferred_element_type=jnp.float32).astype(jnp.bfloat16))
    attended, logsum = lax.map(attend_row, (query, key, value, segment_ids))
    attended = attended.reshape(group, heads_dev * HEAD).astype(jnp.bfloat16)
    hidden = x + lax.psum_scatter(
        jnp.dot(attended, wo, preferred_element_type=jnp.float32),
        "tensor",
        scatter_dimension=0,
        tiled=True,
    )
    normed_hidden, scale_m = norm_forward(hidden, gain_m)
    normed_m = lax.all_gather(normed_hidden.astype(jnp.bfloat16), "tensor", axis=0, tiled=True)
    gate = jnp.dot(normed_m, wg, preferred_element_type=jnp.float32)
    up = jnp.dot(normed_m, wu, preferred_element_type=jnp.float32)
    sigma = jax.nn.sigmoid(gate)
    silu_gate = gate * sigma
    act = (silu_gate * up).astype(jnp.bfloat16)
    output = hidden + lax.psum_scatter(
        jnp.dot(act, wd, preferred_element_type=jnp.float32).astype(jnp.bfloat16),
        "tensor",
        scatter_dimension=0,
        tiled=True,
    ).astype(jnp.float32)
    wq, wk, wv, wo, wg, wu, wd = (
        lax.all_gather(local[0], "fsdp", axis=0, tiled=True),
        lax.all_gather(local[1], "fsdp", axis=0, tiled=True),
        lax.all_gather(local[2], "fsdp", axis=0, tiled=True),
        lax.all_gather(local[3], "fsdp", axis=1, tiled=True),
        lax.all_gather(local[4], "fsdp", axis=0, tiled=True),
        lax.all_gather(local[5], "fsdp", axis=0, tiled=True),
        lax.all_gather(local[6], "fsdp", axis=1, tiled=True),
    )
    grad_all = lax.all_gather(out_grad, "tensor", axis=0, tiled=True)
    grad_down = dot_tn(act, grad_all)
    grad_act = dot_nt(grad_all, wd)
    grad_gate = (grad_act * up * (sigma * (1.0 + gate * (1.0 - sigma)))).astype(jnp.bfloat16)
    grad_up = (grad_act * silu_gate).astype(jnp.bfloat16)
    grad_wgate = dot_tn(normed_m, grad_gate)
    grad_wup = dot_tn(normed_m, grad_up)
    grad_nm = lax.psum_scatter(
        dot_nt(grad_gate, wg) + dot_nt(grad_up, wu), "tensor", scatter_dimension=0, tiled=True
    )
    back_m, gain_m_part = norm_backward(hidden, scale_m, gain_m, grad_nm)
    grad_hidden = out_grad.astype(jnp.float32) + back_m
    grad_hidden_low = grad_hidden.astype(jnp.bfloat16)
    branch_all = lax.all_gather(grad_hidden_low, "tensor", axis=0, tiled=True)
    grad_wout = dot_tn(attended, branch_all)
    grad_attended = heads(dot_nt(branch_all, wo).astype(jnp.bfloat16))
    grad_query, grad_key, grad_value = lax.map(
        attend_back, (query, key, value, segment_ids, logsum, grad_attended)
    )
    grad_qpre = (
        rotate(grad_query, cosine, -sine).reshape(group, heads_dev * HEAD).astype(jnp.bfloat16)
    )
    grad_kpre = (
        rotate(grad_key, cosine, -sine).reshape(group, heads_dev * HEAD).astype(jnp.bfloat16)
    )
    grad_vpre = grad_value.reshape(group, heads_dev * HEAD).astype(jnp.bfloat16)
    grad_wq = dot_tn(normed_a, grad_qpre)
    grad_wk = dot_tn(normed_a, grad_kpre)
    grad_wv = dot_tn(normed_a, grad_vpre)
    grad_na_part = dot_nt(grad_qpre, wq) + dot_nt(grad_kpre, wk) + dot_nt(grad_vpre, wv)
    grad_na = lax.psum_scatter(
        grad_na_part.astype(jnp.bfloat16), "tensor", scatter_dimension=0, tiled=True
    ).astype(jnp.float32)
    back_a, gain_a_part = norm_backward(x, scale_a, gain_a, grad_na)
    tokens_grad = (grad_hidden + back_a).astype(jnp.bfloat16)
    gain_a_grad, gain_m_grad = lax.psum((gain_a_part, gain_m_part), ("fsdp", "tensor"))
    weight_grads = (
        lax.psum_scatter(
            grad_wq.astype(jnp.bfloat16), "fsdp", scatter_dimension=0, tiled=True
        ).astype(jnp.float32),
        lax.psum_scatter(
            grad_wk.astype(jnp.bfloat16), "fsdp", scatter_dimension=0, tiled=True
        ).astype(jnp.float32),
        lax.psum_scatter(
            grad_wv.astype(jnp.bfloat16), "fsdp", scatter_dimension=0, tiled=True
        ).astype(jnp.float32),
        lax.psum_scatter(
            grad_wout.astype(jnp.bfloat16), "fsdp", scatter_dimension=1, tiled=True
        ).astype(jnp.float32),
        lax.psum_scatter(
            grad_wgate.astype(jnp.bfloat16), "fsdp", scatter_dimension=0, tiled=True
        ).astype(jnp.float32),
        lax.psum_scatter(
            grad_wup.astype(jnp.bfloat16), "fsdp", scatter_dimension=0, tiled=True
        ).astype(jnp.float32),
        lax.psum_scatter(
            grad_down.astype(jnp.bfloat16), "fsdp", scatter_dimension=1, tiled=True
        ).astype(jnp.float32),
    )
    return (
        output.astype(jnp.bfloat16),
        tokens_grad,
        gain_a_grad,
        gain_m_grad,
        weight_grads[0],
        weight_grads[1],
        weight_grads[2],
        weight_grads[3],
        weight_grads[4],
        weight_grads[5],
        weight_grads[6],
    )


def solution(mesh):
    return jax.shard_map(
        shards,
        mesh=mesh,
        in_specs=(
            P(("fsdp", "tensor"), None),
            P(),
            P(),
            P("fsdp", "tensor"),
            P("fsdp", "tensor"),
            P("fsdp", "tensor"),
            P("tensor", "fsdp"),
            P("fsdp", "tensor"),
            P("fsdp", "tensor"),
            P("tensor", "fsdp"),
            P("fsdp", None),
            P(("fsdp", "tensor"), None),
        ),
        out_specs=(
            P(("fsdp", "tensor"), None),
            P(("fsdp", "tensor"), None),
            P(),
            P(),
            P("fsdp", "tensor"),
            P("fsdp", "tensor"),
            P("fsdp", "tensor"),
            P("tensor", "fsdp"),
            P("fsdp", "tensor"),
            P("fsdp", "tensor"),
            P("tensor", "fsdp"),
        ),
        check_vma=False,
    )
```

profile of v0, /device:TPU:0, one launch (start us, length us, event | category | flops | bytes accessed | tf_op | source)
XLA Modules:
  0.0 1231.1 jit_solution(9686080261791631921)
XLA Ops:
  20.3 20.0 %all-gather.18.cloned.1.call-done = bf16[2048,256]{1,0:T(8,128)(2,1)} async-done(((bf16[512,256]{1,0:T(8,128)(2,1)}), bf16[2048,256]{1,0:T(8,128)(2,1)}) %all-gather.18.cloned.1.call-update) | async-done | bytes 1048592 | tf_op jit(solution)/shard_map/all_gather | solution.py:122
  40.3 43.0 %all-gather.12.cloned.1.call-done = bf16[1280,2048]{1,0:T(8,128)(2,1)} async-done(((bf16[160,2048]{1,0:T(8,128)(2,1)}), bf16[1280,2048]{1,0:T(8,128)(2,1)}) %all-gather.12.cloned.1.call-update) | async-done | bytes 5242896 | tf_op jit(solution)/shard_map/all_gather | solution.py:141
  87.7 25.2 %all-gather.16.cloned.1.call-done = bf16[2048,256]{1,0:T(8,128)(2,1)} async-done(((bf16[512,256]{1,0:T(8,128)(2,1)}), bf16[2048,256]{1,0:T(8,128)(2,1)}) %all-gather.16.cloned.1.call-update) | async-done | bytes 1048592 | tf_op jit(solution)/shard_map/all_gather | solution.py:121
  117.6 11.1 fusion.39
  128.8 10.6 fusion.1
  146.1 21.8 %fusion.14 = bf16[4,64,1280]{2,1,0:T(8,128)(2,1)S(1)} fusion(bf16[1280,4,64]{0,2,1:T(8,128)(2,1)S(1)} %bitcast.97, f32[4,1280,1280]{1,2,0:T(8,128)} %get-tuple-element.91, f32[4,1280]{1,0:T(4,128)S(1)} %fusion.1, f32[4,1280]{1,0:T(4,128)S(1)} %get-tuple-element.90), kind=kOutput, calls=%fused_computation.41 | convolution fusion | flops 858849280 | bytes 27566080 | tf_op jit(solution)/shard_map/while/body/eval_jaxpr/hqk,khd->qhd/dot_general | solution.py:80
  178.2 80.4 %reduce-scatter.12.cloned.1.call-done = f32[160,2048]{1,0:T(8,128)} async-done(((f32[1280,2048]{1,0:T(8,128)}), f32[160,2048]{1,0:T(8,128)}) %reduce-scatter.12.cloned.1.call-update) | async-done | bytes 1310736 | tf_op jit(solution)/shard_map/reduce_scatter | solution.py:151
  263.3 77.6 %all-gather.26.cloned.1.call-done = bf16[2048,1024]{1,0:T(8,128)(2,1)} async-done(((bf16[512,1024]{1,0:T(8,128)(2,1)}), bf16[2048,1024]{1,0:T(8,128)(2,1)}) %all-gather.26.cloned.1.call-update) | async-done | bytes 4194320 | tf_op jit(solution)/shard_map/all_gather | solution.py:126
  340.9 42.1 %all-gather.22.cloned.1.call-done = bf16[1280,2048]{1,0:T(8,128)(2,1)} async-done(((bf16[160,2048]{1,0:T(8,128)(2,1)}), bf16[1280,2048]{1,0:T(8,128)(2,1)}) %all-gather.22.cloned.1.call-update) | async-done | bytes 5242896 | tf_op jit(solution)/shard_map/all_gather | solution.py:158
  383.0 10.2 fusion.44
  393.3 72.2 %all-gather.24.cloned.1.call-done = bf16[2048,1024]{1,0:T(8,128)(2,1)} async-done(((bf16[512,1024]{1,0:T(8,128)(2,1)}), bf16[2048,1024]{1,0:T(8,128)(2,1)}) %all-gather.24.cloned.1.call-update) | async-done | bytes 4194320 | tf_op jit(solution)/shard_map/all_gather | solution.py:125
  465.4 10.2 fusion.43
  475.6 70.5 %all-gather.28.cloned.1.call-done = bf16[1024,2048]{1,0:T(8,128)(2,1)} async-done(((bf16[1024,512]{1,0:T(8,128)(2,1)}), bf16[1024,2048]{1,0:T(8,128)(2,1)}) %all-gather.28.cloned.1.call-update) | async-done | bytes 4194320 | tf_op jit(solution)/shard_map/all_gather | solution.py:127
  546.2 41.6 %all-gather.30.cloned.1.call-done = bf16[1280,2048]{1,0:T(8,128)(2,1)} async-done(((bf16[160,2048]{1,0:T(8,128)(2,1)}), bf16[1280,2048]{1,0:T(8,128)(2,1)}) %all-gather.30.cloned.1.call-update) | async-done | bytes 5242896 | tf_op jit(solution)/shard_map/all_gather | solution.py:179
  587.7 14.7 %multiply_convert_fusion.1 = (bf16[1280,1024]{1,0:T(8,128)(2,1)S(1)}, bf16[1280,1024]{1,0:T(8,128)(2,1)S(1)}, bf16[1280,1024]{1,0:T(8,128)(2,1)}) fusion(f32[1280,1024]{1,0:T(8,128)} %fusion.43, f32[1280,1024]{1,0:T(8,128)} %fusion.44, bf16[1280,2048]{1,0:T(8,128)(2,1)} %all-gather.30.cloned.1.call-done, bf16[1024,2048]{1,0:T(8,128)(2,1)} %all-gather.28.cloned.1.call-done), kind=kOutput, calls=%fused_computation.17 | convolution fusion | flops 5388369920 | bytes 27787264 | tf_op jit(solution)/shard_map/dot_general | solution.py:13
  610.7 11.0 convolution_add_fusion
  621.7 81.7 %reduce-scatter.16.cloned.1.call-done = f32[160,2048]{1,0:T(8,128)} async-done(((f32[1280,2048]{1,0:T(8,128)}), f32[160,2048]{1,0:T(8,128)}) %reduce-scatter.16.cloned.1.call-update) | async-done | bytes 1310736 | tf_op jit(solution)/shard_map/reduce_scatter | solution.py:186
  718.0 10.2 convolution_convert_fusion.2
  728.2 10.2 convolution_convert_fusion.3
  738.9 10.1 all-gather.32.cloned.1.call-done
  758.4 10.8 fusion.11
  774.3 16.7 %multiply_reduce_fusion = (f32[4,1280]{1,0:T(4,128)S(1)}, f32[4,1280,1280]{1,2,0:T(8,128)}) fusion(f32[4,1280,1280]{1,2,0:T(8,128)} %get-tuple-element.91, f32[4,1280]{1,0:T(4,128)S(1)} %log_add_fusion, bf16[1280,4,64]{0,2,1:T(8,128)(2,1)S(1)} %bitcast.90, bf16[1280,4,64]{0,2,1:T(8,128)(2,1)S(1)} %bitcast.98), kind=kOutput, calls=%fused_computation.3 | convolution fusion | flops 858516480 | bytes 53780480 | tf_op jit(solution)/shard_map/while/body/eval_jaxpr/qhd,khd->hqk/dot_general | solution.py:91
  791.2 22.5 %multiply_convert_fusion = bf16[4,1280,1280]{1,2,0:T(8,128)(2,1)} fusion(f32[4,1280,1280]{1,2,0:T(8,128)} %get-tuple-element.93, f32[4,1280,1280]{1,2,0:T(8,128)} %get-tuple-element.91, f32[4,1280]{1,0:T(4,128)S(1)} %get-tuple-element.92, f32[4,1280]{1,0:T(4,128)S(1)} %log_add_fusion), kind=kLoop, calls=%fused_computation.2 | loop fusion | flops 26214400 | bytes 65576960 | tf_op jit(solution)/shard_map/while/body/eval_jaxpr/convert_element_type | solution.py:93
  868.5 39.0 %reduce-scatter.30.cloned.1.call-done = bf16[512,1024]{1,0:T(8,128)(2,1)} async-done(((bf16[2048,1024]{1,0:T(8,128)(2,1)}), bf16[512,1024]{1,0:T(8,128)(2,1)}) %reduce-scatter.30.cloned.1.call-update) | async-done | bytes 1048592 | tf_op jit(solution)/shard_map/reduce_scatter | solution.py:231
  910.3 76.6 %reduce-scatter.28.cloned.1.call-done = bf16[512,1024]{1,0:T(8,128)(2,1)} async-done(((bf16[2048,1024]{1,0:T(8,128)(2,1)}), bf16[512,1024]{1,0:T(8,128)(2,1)}) %reduce-scatter.28.cloned.1.call-update) | async-done | bytes 1048592 | tf_op jit(solution)/shard_map/reduce_scatter | solution.py:228
  989.7 27.2 %reduce-scatter.26.cloned.1.call-done = bf16[256,512]{1,0:T(8,128)(2,1)} async-done(((bf16[256,2048]{1,0:T(8,128)(2,1)}), bf16[256,512]{1,0:T(8,128)(2,1)}) %reduce-scatter.26.cloned.1.call-update) | async-done | bytes 262160 | tf_op jit(solution)/shard_map/reduce_scatter | solution.py:225
  1018.7 26.1 %reduce-scatter.24.cloned.1.call-done = bf16[512,256]{1,0:T(8,128)(2,1)} async-done(((bf16[2048,256]{1,0:T(8,128)(2,1)}), bf16[512,256]{1,0:T(8,128)(2,1)}) %reduce-scatter.24.cloned.1.call-update) | async-done | bytes 262160 | tf_op jit(solution)/shard_map/reduce_scatter | solution.py:222
  1046.6 26.5 %reduce-scatter.22.cloned.1.call-done = bf16[512,256]{1,0:T(8,128)(2,1)} async-done(((bf16[2048,256]{1,0:T(8,128)(2,1)}), bf16[512,256]{1,0:T(8,128)(2,1)}) %reduce-scatter.22.cloned.1.call-update) | async-done | bytes 262160 | tf_op jit(solution)/shard_map/reduce_scatter | solution.py:219
  1074.9 26.2 %reduce-scatter.20.cloned.1.call-done = bf16[512,256]{1,0:T(8,128)(2,1)} async-done(((bf16[2048,256]{1,0:T(8,128)(2,1)}), bf16[512,256]{1,0:T(8,128)(2,1)}) %reduce-scatter.20.cloned.1.call-update) | async-done | bytes 262160 | tf_op jit(solution)/shard_map/reduce_scatter | solution.py:216
  1102.8 57.3 %reduce-scatter.18.cloned.1.call-done = bf16[160,2048]{1,0:T(8,128)(2,1)} async-done(((bf16[1280,2048]{1,0:T(8,128)(2,1)}), bf16[160,2048]{1,0:T(8,128)(2,1)}) %reduce-scatter.18.cloned.1.call-update) | async-done | bytes 655376 | tf_op jit(solution)/shard_map/reduce_scatter | solution.py:209
  1161.6 39.8 %all-reduce = (f32[2048]{0:T(1024)}, f32[2048]{0:T(1024)}) all-reduce(f32[2048]{0:T(1024)S(1)} %get-tuple-element.54, f32[2048]{0:T(1024)S(1)} %get-tuple-element.52), channel_id=1, replica_groups=mesh['fsdp'=4,'tensor'=8] {'fsdp','tensor'}, use_global_device_ids=true, to_apply=%region_14.15 | all-reduce | flops 4096 | bytes 32768 | tf_op jit(solution)/shard_map/psum | solution.py:214
  1201.4 19.3 %reduce-scatter.14.cloned.1.call-done = bf16[160,2048]{1,0:T(8,128)(2,1)} async-done(((bf16[1280,2048]{1,0:T(8,128)(2,1)}), bf16[160,2048]{1,0:T(8,128)(2,1)}) %reduce-scatter.14.cloned.1.call-update) | async-done | bytes 655376 | tf_op jit(solution)/shard_map/reduce_scatter | solution.py:164
  (159 shorter events, 153.9 us)
Async XLA Ops:
  7.2 33.1 %all-gather.18.cloned.1.call-start = ((), (), s32[]{:S(2)}) async-start(), calls=%async_computation.14 | async-start | bytes 1310720 | tf_op jit(solution)/shard_map/all_gather | solution.py:122
  7.9 75.4 %all-gather.12.cloned.1.call-start = ((), (), s32[]{:S(2)}) async-start(), calls=%async_computation.11 | async-start | bytes 5898240 | tf_op jit(solution)/shard_map/all_gather | solution.py:141
  12.7 100.2 %all-gather.16.cloned.1.call-start = ((), (), s32[]{:S(2)}) async-start(), calls=%async_computation.13 | async-start | bytes 1310720 | tf_op jit(solution)/shard_map/all_gather | solution.py:121
  13.4 128.3 %all-gather.14.cloned.1.call-start = ((), (), s32[]{:S(2)}) async-start(), calls=%async_computation.12 | async-start | bytes 1310720 | tf_op jit(solution)/shard_map/all_gather | solution.py:123
  14.0 156.6 %all-gather.20.cloned.1.call-start = ((), (), s32[]{:S(2)}) async-start(), calls=%async_computation.15 | async-start | bytes 1310720 | tf_op jit(solution)/shard_map/all_gather | solution.py:124
  14.6 243.9 %reduce-scatter.12.cloned.1.call-start = ((), (), s32[]{:S(2)}) async-start(), calls=%async_computation.16 | async-start | bytes 11796480 | tf_op jit(solution)/shard_map/reduce_scatter | solution.py:151
  20.3 97.0 %copy-start.4 = (f32[1280,32]{0,1:T(8,128)}, f32[1280,32]{0,1:T(8,128)S(1)}, u32[]{:S(2)}) copy-start(f32[1280,32]{0,1:T(8,128)S(1)} %get-tuple-element.89) | copy-start | bytes 491524
  177.3 81.2 %copy-start = (bf16[160,2048]{1,0:T(8,128)(2,1)S(1)}, bf16[160,2048]{1,0:T(8,128)(2,1)}, u32[]{:S(2)}) copy-start(bf16[160,2048]{1,0:T(8,128)(2,1)} %param.12) | copy-start | bytes 1966084
  177.4 163.5 %all-gather.26.cloned.1.call-start = ((), (), s32[]{:S(2)}) async-start(), calls=%async_computation.19 | async-start | bytes 5242880 | tf_op jit(solution)/shard_map/all_gather | solution.py:126
  178.1 204.9 %all-gather.22.cloned.1.call-start = ((), (), s32[]{:S(2)}) async-start(), calls=%async_computation.17 | async-start | bytes 5898240 | tf_op jit(solution)/shard_map/all_gather | solution.py:158
  261.2 204.2 %all-gather.24.cloned.1.call-start = ((), (), s32[]{:S(2)}) async-start(), calls=%async_computation.18 | async-start | bytes 5242880 | tf_op jit(solution)/shard_map/all_gather | solution.py:125
  261.9 284.2 %all-gather.28.cloned.1.call-start = ((), (), s32[]{:S(2)}) async-start(), calls=%async_computation.20 | async-start | bytes 5242880 | tf_op jit(solution)/shard_map/all_gather | solution.py:127
  262.5 325.2 %all-gather.30.cloned.1.call-start = ((), (), s32[]{:S(2)}) async-start(), calls=%async_computation.22 | async-start | bytes 5898240 | tf_op jit(solution)/shard_map/all_gather | solution.py:179
  263.2 440.2 %reduce-scatter.16.cloned.1.call-start = ((), (), s32[]{:S(2)}) async-start(), calls=%async_computation.23 | async-start | bytes 11796480 | tf_op jit(solution)/shard_map/reduce_scatter | solution.py:186
  621.7 83.4 %copy-start.3 = (bf16[160,2048]{1,0:T(8,128)(2,1)S(1)}, bf16[160,2048]{1,0:T(8,128)(2,1)}, u32[]{:S(2)}) copy-start(bf16[160,2048]{1,0:T(8,128)(2,1)} %param.23) | copy-start | bytes 1966084
  621.7 127.3 %all-gather.32.cloned.1.call-start = ((), (), s32[]{:S(2)}) async-start(), calls=%async_computation.24 | async-start | bytes 5898240 | tf_op jit(solution)/shard_map/all_gather | solution.py:192
  707.8 157.9 %reduce-scatter.32.cloned.1.call-start = ((), (), s32[]{:S(2)}) async-start(), calls=%async_computation.32 | async-start | bytes 5242880 | tf_op jit(solution)/shard_map/reduce_scatter | solution.py:234
  717.9 189.6 %reduce-scatter.30.cloned.1.call-start = ((), (), s32[]{:S(2)}) async-start(), calls=%async_computation.31 | async-start | bytes 5242880 | tf_op jit(solution)/shard_map/reduce_scatter | solution.py:231
  728.2 258.8 %reduce-scatter.28.cloned.1.call-start = ((), (), s32[]{:S(2)}) async-start(), calls=%async_computation.30 | async-start | bytes 5242880 | tf_op jit(solution)/shard_map/reduce_scatter | solution.py:228
  738.4 278.4 %reduce-scatter.26.cloned.1.call-start = ((), (), s32[]{:S(2)}) async-start(), calls=%async_computation.29 | async-start | bytes 1310720 | tf_op jit(solution)/shard_map/reduce_scatter | solution.py:225
  754.0 290.8 %reduce-scatter.24.cloned.1.call-start = ((), (), s32[]{:S(2)}) async-start(), calls=%async_computation.28 | async-start | bytes 1310720 | tf_op jit(solution)/shard_map/reduce_scatter | solution.py:222
  791.0 282.1 %reduce-scatter.22.cloned.1.call-start = ((), (), s32[]{:S(2)}) async-start(), calls=%async_computation.27 | async-start | bytes 1310720 | tf_op jit(solution)/shard_map/reduce_scatter | solution.py:219
  791.2 22.5 %copy-start.11 = (bf16[1280,4,32]{0,2,1:T(8,128)(2,1)S(1)}, bf16[1280,4,32]{0,2,1:T(8,128)(2,1)}, u32[]{:S(2)}) copy-start(bf16[1280,4,32]{0,2,1:T(8,128)(2,1)} %copy-done.10) | copy-start | bytes 983044
  791.2 22.5 %copy-start.13 = (bf16[1280,4,32]{0,2,1:T(8,128)(2,1)S(1)}, bf16[1280,4,32]{0,2,1:T(8,128)(2,1)}, u32[]{:S(2)}) copy-start(bf16[1280,4,32]{0,2,1:T(8,128)(2,1)} %copy-done.12) | copy-start | bytes 983044
  813.7 16.7 %slice-start = ((s8[5242880]{0:T(1024)(128)(4,1)}), s8[1048576]{0:T(1024)(128)(4,1)S(1)}, s32[]{:S(2)}) async-start(s8[5242880]{0:T(1024)(128)(4,1)} %bitcast.104), calls=%async_computation.33 | async-start | bytes 2097152
  833.1 267.9 %reduce-scatter.20.cloned.1.call-start = ((), (), s32[]{:S(2)}) async-start(), calls=%async_computation.26 | async-start | bytes 1310720 | tf_op jit(solution)/shard_map/reduce_scatter | solution.py:216
  838.3 321.8 %reduce-scatter.18.cloned.1.call-start = ((), (), s32[]{:S(2)}) async-start(), calls=%async_computation.25 | async-start | bytes 5898240 | tf_op jit(solution)/shard_map/reduce_scatter | solution.py:209
  855.5 365.1 %reduce-scatter.14.cloned.1.call-start = ((), (), s32[]{:S(2)}) async-start(), calls=%async_computation.21 | async-start | bytes 5898240 | tf_op jit(solution)/shard_map/reduce_scatter | solution.py:164
  868.5 291.6 %copy-start.1 = (bf16[160,2048]{1,0:T(8,128)(2,1)S(1)}, bf16[160,2048]{1,0:T(8,128)(2,1)}, u32[]{:S(2)}) copy-start(bf16[160,2048]{1,0:T(8,128)(2,1)} %param.12) | copy-start | bytes 1966084
  868.5 291.6 %copy-start.18 = (f32[2048]{0:T(1024)S(1)}, f32[2048]{0:T(1024)}, u32[]{:S(2)}) copy-start(f32[2048]{0:T(1024)} %copy-done.17) | copy-start | bytes 24580
  868.5 291.6 %copy-start.20 = (f32[160]{0:T(256)S(1)}, f32[160]{0:T(256)}, u32[]{:S(2)}) copy-start(f32[160]{0:T(256)} %copy-done.19) | copy-start | bytes 1924
  910.3 310.4 %copy-start.2 = (f32[160,2048]{1,0:T(8,128)S(1)}, f32[160,2048]{1,0:T(8,128)}, u32[]{:S(2)}) copy-start(f32[160,2048]{1,0:T(8,128)} %reduce-scatter.16.cloned.1.call-done) | copy-start | bytes 3932164
  (18 other events, 135.5 us)
Sparse Core Ops, SparseCore 0:
  9.6 30.6 all-gather.17
  42.8 40.5 all-gather.11
  84.9 27.9 all-gather.15
  114.3 27.4 all-gather.13
  143.2 27.4 all-gather.19
  177.5 81.0 reduce-scatter.11
  260.1 80.7 all-gather.25
  343.4 39.6 all-gather.21
  384.6 80.7 all-gather.23
  466.8 79.2 all-gather.27
  548.0 39.6 all-gather.29
  621.8 81.5 reduce-scatter.15
  707.9 41.0 all-gather.31
  751.2 76.7 reduce-scatter.31
  830.2 77.2 reduce-scatter.29
  909.7 77.2 reduce-scatter.27
  989.2 27.6 reduce-scatter.25
  1019.0 25.7 reduce-scatter.23
  1047.2 25.8 reduce-scatter.21
  1075.2 25.7 reduce-scatter.19
  1104.8 55.2 reduce-scatter.17
  1163.5 57.1 reduce-scatter.13
where the time goes:
time: 1240 us; the launch traced here: 1230 us
  waiting for transfers between devices  873 us (70%)
  matrix products  230 us (19%)
  other arithmetic  70.7 us (6%)
  blocking collectives  39.8 us (3%)
  between operations  15 us (1%)
    reduce_scatter x1, waiting for transfers between devices, shards(): lax.psum_scatter(dot_nt(grad_gate, wg) + dot_nt(grad_up, wu), 'tensor', s...  81.7 us
    reduce_scatter x1, waiting for transfers between devices, shards(): lax.psum_scatter(jnp.dot(attended, wo, preferred_element_type=jnp.float32...  80.4 us
    all_gather x1, waiting for transfers between devices, shards(): lax.all_gather(local[5], 'fsdp', axis=0, tiled=True)  77.6 us
    reduce_scatter x1, waiting for transfers between devices, shards(): lax.psum_scatter(grad_wgate.astype(jnp.bfloat16), 'fsdp', scatter_dimensi...  76.6 us
    all_gather x1, waiting for transfers between devices, shards(): lax.all_gather(local[4], 'fsdp', axis=0, tiled=True)  72.2 us
    all_gather x1, waiting for transfers between devices, shards(): lax.all_gather(local[6], 'fsdp', axis=1, tiled=True)  70.5 us
    reduce_scatter x1, waiting for transfers between devices, shards(): lax.psum_scatter(grad_na_part.astype(jnp.bfloat16), 'tensor', scatter_dim...  57.3 us
    dot_general x7, matrix products, dot_nt(): lax.dot_general(left, right, (((1,), (1,)), ((), ())), preferred_element_...  55.2 us
  transfers between devices with their start and end apart: 22, of which 21 were waited for; matrix products, arithmetic and copies ran while one was open for 21% of the time, Pallas kernels for 0%

commit v1 on v0

--- a/solution.py
+++ b/solution.py
@@ -176,7 +176,14 @@
         lax.all_gather(local[5], "fsdp", axis=0, tiled=True),
         lax.all_gather(local[6], "fsdp", axis=1, tiled=True),
     )
-    grad_all = lax.all_gather(out_grad, "tensor", axis=0, tiled=True)
+    ring = [out_grad]
+    for hop in range(7):
+        ring.append(lax.ppermute(ring[-1], "tensor", [(dev, (dev + 1) % 8) for dev in range(8)]))
+    grad_all = jnp.roll(
+        jnp.concatenate(ring[::-1], axis=0),
+        (lax.axis_index("tensor") + 1) * ring[0].shape[0],
+        axis=0,
+    )
     grad_down = dot_tn(act, grad_all)
     grad_act = dot_nt(grad_all, wd)
     grad_gate = (grad_act * up * (sigma * (1.0 + gate * (1.0 - sigma)))).astype(jnp.bfloat16)

time: 1240 us -> 1200 us (0.968)
  waiting for transfers between devices: 873 us -> 805 us
  local copies, waits for them, and re-layouts: 0.97 us -> 25.6 us
    all_gather x1, waiting for transfers between devices: 77.6 us -> 0.01 us  [shards(): lax.all_gather(local[5], 'fsdp', axis=0, tiled=True)]
    ppermute x0 -> x7, waiting for transfers between devices: none -> 76.6 us  [shards(): lax.ppermute(ring[-1], 'tensor', [(dev, (dev + 1) % 8) for dev in range(8)])]
    all_gather x1 -> x0, waiting for transfers between devices: 41.6 us -> none  [shards(): grad_all = lax.all_gather(out_grad, 'tensor', axis=0, tiled=True)]
    unnamed x56 -> x93, local copies, waits for them, and re-layouts: 0.68 us -> 24.4 us
    all_gather x1, waiting for transfers between devices: 42.1 us -> 20.4 us  [shards(): lax.all_gather(normed_hidden.astype(jnp.bfloat16), 'tensor', axis=0, tile...]
  transfers between devices with their start and end apart: 22 -> 28, of which waited for: 21 -> 26; matrix products, arithmetic and copies ran while one was open for 21% -> 23% of each run, Pallas kernels for 0% -> 0%
where the time goes in v1:
time: 1200 us; the launch traced here: 1190 us
  waiting for transfers between devices  805 us (67%)
  matrix products  230 us (19%)
  other arithmetic  70.7 us (6%)
  blocking collectives  39.8 us (3%)
  local copies, waits for them, and re-layouts  25.6 us (2%)
  between operations  15.3 us (1%)
    reduce_scatter x1, waiting for transfers between devices, shards(): lax.psum_scatter(jnp.dot(attended, wo, preferred_element_type=jnp.float32...  80.4 us
    reduce_scatter x1, waiting for transfers between devices, shards(): lax.psum_scatter(dot_nt(grad_gate, wg) + dot_nt(grad_up, wu), 'tensor', s...  80.2 us
    reduce_scatter x1, waiting for transfers between devices, shards(): lax.psum_scatter(grad_wgate.astype(jnp.bfloat16), 'fsdp', scatter_dimensi...  76.7 us
    ppermute x7, waiting for transfers between devices, shards(): lax.ppermute(ring[-1], 'tensor', [(dev, (dev + 1) % 8) for dev in range(8)])  76.6 us
    all_gather x1, waiting for transfers between devices, shards(): lax.all_gather(local[4], 'fsdp', axis=0, tiled=True)  72.1 us
    all_gather x1, waiting for transfers between devices, shards(): lax.all_gather(local[6], 'fsdp', axis=1, tiled=True)  70.5 us
    reduce_scatter x1, waiting for transfers between devices, shards(): lax.psum_scatter(grad_na_part.astype(jnp.bfloat16), 'tensor', scatter_dim...  57.1 us
    dot_general x7, matrix products, dot_nt(): lax.dot_general(left, right, (((1,), (1,)), ((), ())), preferred_element_...  54.5 us
  transfers between devices with their start and end apart: 28, of which 26 were waited for; matrix products, arithmetic and copies ran while one was open for 23% of the time, Pallas kernels for 0%

profile of v1, /device:TPU:0, one launch (start us, length us, event | category | flops | bytes accessed | tf_op | source)
XLA Modules:
  0.0 1188.0 jit_solution(4787386813413187008)
XLA Ops:
  20.3 20.0 %all-gather.17.cloned.1.call-done = bf16[2048,256]{1,0:T(8,128)(2,1)} async-done(((bf16[512,256]{1,0:T(8,128)(2,1)}), bf16[2048,256]{1,0:T(8,128)(2,1)}) %all-gather.17.cloned.1.call-update) | async-done | bytes 1048592 | tf_op jit(solution)/shard_map/all_gather | solution.py:122
  40.3 43.0 %all-gather.11.cloned.1.call-done = bf16[1280,2048]{1,0:T(8,128)(2,1)} async-done(((bf16[160,2048]{1,0:T(8,128)(2,1)}), bf16[1280,2048]{1,0:T(8,128)(2,1)}) %all-gather.11.cloned.1.call-update) | async-done | bytes 5242896 | tf_op jit(solution)/shard_map/all_gather | solution.py:141
  87.7 25.2 %all-gather.15.cloned.1.call-done = bf16[2048,256]{1,0:T(8,128)(2,1)} async-done(((bf16[512,256]{1,0:T(8,128)(2,1)}), bf16[2048,256]{1,0:T(8,128)(2,1)}) %all-gather.15.cloned.1.call-update) | async-done | bytes 1048592 | tf_op jit(solution)/shard_map/all_gather | solution.py:121
  117.6 11.1 fusion.48
  128.7 10.6 fusion.1
  147.0 22.7 %fusion.21 = bf16[4,64,1280]{2,1,0:T(8,128)(2,1)S(1)} fusion(bf16[1280,4,64]{0,2,1:T(8,128)(2,1)S(1)} %bitcast.95, f32[4,1280,1280]{1,2,0:T(8,128)} %get-tuple-element.91, f32[4,1280]{1,0:T(4,128)S(1)} %fusion.1, f32[4,1280]{1,0:T(4,128)S(1)} %get-tuple-element.90), kind=kOutput, calls=%fused_computation.45 | convolution fusion | flops 858849280 | bytes 27566080 | tf_op jit(solution)/shard_map/while/body/eval_jaxpr/hqk,khd->qhd/dot_general | solution.py:80
  178.2 80.4 %reduce-scatter.12.cloned.1.call-done = f32[160,2048]{1,0:T(8,128)} async-done(((f32[1280,2048]{1,0:T(8,128)}), f32[160,2048]{1,0:T(8,128)}) %reduce-scatter.12.cloned.1.call-update) | async-done | bytes 1310736 | tf_op jit(solution)/shard_map/reduce_scatter | solution.py:151
  262.1 10.9 collective-permute-done
  273.0 10.9 collective-permute-done.1
  283.9 10.9 collective-permute-done.2
  295.6 10.9 collective-permute-done.3
  307.4 10.9 collective-permute-done.4
  319.1 11.0 collective-permute-done.5
  330.2 11.1 collective-permute-done.6
  362.7 20.4 %all-gather.21.cloned.1.call-done = bf16[1280,2048]{1,0:T(8,128)(2,1)} async-done(((bf16[160,2048]{1,0:T(8,128)(2,1)}), bf16[1280,2048]{1,0:T(8,128)(2,1)}) %all-gather.21.cloned.1.call-update) | async-done | bytes 5242896 | tf_op jit(solution)/shard_map/all_gather | solution.py:158
  393.3 72.1 %all-gather.23.cloned.1.call-done = bf16[2048,1024]{1,0:T(8,128)(2,1)} async-done(((bf16[512,1024]{1,0:T(8,128)(2,1)}), bf16[2048,1024]{1,0:T(8,128)(2,1)}) %all-gather.23.cloned.1.call-update) | async-done | bytes 4194320 | tf_op jit(solution)/shard_map/all_gather | solution.py:125
  475.7 70.5 %all-gather.27.cloned.1.call-done = bf16[1024,2048]{1,0:T(8,128)(2,1)} async-done(((bf16[1024,512]{1,0:T(8,128)(2,1)}), bf16[1024,2048]{1,0:T(8,128)(2,1)}) %all-gather.27.cloned.1.call-update) | async-done | bytes 4194320 | tf_op jit(solution)/shard_map/all_gather | solution.py:127
  546.2 14.0 %multiply_convert_fusion.1 = (bf16[1280,1024]{1,0:T(8,128)(2,1)S(1)}, bf16[1280,1024]{1,0:T(8,128)(2,1)S(1)}, bf16[1280,1024]{1,0:T(8,128)(2,1)}) fusion(f32[1280,1024]{1,0:T(8,128)} %fusion.52, f32[1280,1024]{1,0:T(8,128)} %fusion.53, bf16[1024,2048]{1,0:T(8,128)(2,1)} %all-gather.27.cloned.1.call-done, ...), kind=kOutput, calls=%fused_computation.17 | convolution fusion | flops 5388369920 | bytes 27787268 | tf_op jit(solution)/shard_map/dot_general | solution.py:13
  568.6 11.3 convolution_add_fusion
  579.9 80.2 %reduce-scatter.16.cloned.1.call-done = f32[160,2048]{1,0:T(8,128)} async-done(((f32[1280,2048]{1,0:T(8,128)}), f32[160,2048]{1,0:T(8,128)}) %reduce-scatter.16.cloned.1.call-update) | async-done | bytes 1310736 | tf_op jit(solution)/shard_map/reduce_scatter | solution.py:193
  714.8 10.8 fusion.18
  730.7 16.7 %multiply_reduce_fusion = (f32[4,1280]{1,0:T(4,128)S(1)}, f32[4,1280,1280]{1,2,0:T(8,128)}) fusion(f32[4,1280,1280]{1,2,0:T(8,128)} %get-tuple-element.91, f32[4,1280]{1,0:T(4,128)S(1)} %log_add_fusion, bf16[1280,4,64]{0,2,1:T(8,128)(2,1)S(1)} %bitcast.88, bf16[1280,4,64]{0,2,1:T(8,128)(2,1)S(1)} %bitcast.96), kind=kOutput, calls=%fused_computation.3 | convolution fusion | flops 858516480 | bytes 53780480 | tf_op jit(solution)/shard_map/while/body/eval_jaxpr/qhd,khd->hqk/dot_general | solution.py:91
  747.7 22.4 %multiply_convert_fusion = bf16[4,1280,1280]{1,2,0:T(8,128)(2,1)} fusion(f32[4,1280,1280]{1,2,0:T(8,128)} %get-tuple-element.93, f32[4,1280,1280]{1,2,0:T(8,128)} %get-tuple-element.91, f32[4,1280]{1,0:T(4,128)S(1)} %get-tuple-element.92, f32[4,1280]{1,0:T(4,128)S(1)} %log_add_fusion), kind=kLoop, calls=%fused_computation.2 | loop fusion | flops 26214400 | bytes 65576960 | tf_op jit(solution)/shard_map/while/body/eval_jaxpr/convert_element_type | solution.py:93
  824.9 39.4 %reduce-scatter.30.cloned.1.call-done = bf16[512,1024]{1,0:T(8,128)(2,1)} async-done(((bf16[2048,1024]{1,0:T(8,128)(2,1)}), bf16[512,1024]{1,0:T(8,128)(2,1)}) %reduce-scatter.30.cloned.1.call-update) | async-done | bytes 1048592 | tf_op jit(solution)/shard_map/reduce_scatter | solution.py:238
  867.1 76.7 %reduce-scatter.28.cloned.1.call-done = bf16[512,1024]{1,0:T(8,128)(2,1)} async-done(((bf16[2048,1024]{1,0:T(8,128)(2,1)}), bf16[512,1024]{1,0:T(8,128)(2,1)}) %reduce-scatter.28.cloned.1.call-update) | async-done | bytes 1048592 | tf_op jit(solution)/shard_map/reduce_scatter | solution.py:235
  946.6 27.1 %reduce-scatter.26.cloned.1.call-done = bf16[256,512]{1,0:T(8,128)(2,1)} async-done(((bf16[256,2048]{1,0:T(8,128)(2,1)}), bf16[256,512]{1,0:T(8,128)(2,1)}) %reduce-scatter.26.cloned.1.call-update) | async-done | bytes 262160 | tf_op jit(solution)/shard_map/reduce_scatter | solution.py:232
  975.5 26.2 %reduce-scatter.24.cloned.1.call-done = bf16[512,256]{1,0:T(8,128)(2,1)} async-done(((bf16[2048,256]{1,0:T(8,128)(2,1)}), bf16[512,256]{1,0:T(8,128)(2,1)}) %reduce-scatter.24.cloned.1.call-update) | async-done | bytes 262160 | tf_op jit(solution)/shard_map/reduce_scatter | solution.py:229
  1003.4 26.3 %reduce-scatter.22.cloned.1.call-done = bf16[512,256]{1,0:T(8,128)(2,1)} async-done(((bf16[2048,256]{1,0:T(8,128)(2,1)}), bf16[512,256]{1,0:T(8,128)(2,1)}) %reduce-scatter.22.cloned.1.call-update) | async-done | bytes 262160 | tf_op jit(solution)/shard_map/reduce_scatter | solution.py:226
  1031.5 26.3 %reduce-scatter.20.cloned.1.call-done = bf16[512,256]{1,0:T(8,128)(2,1)} async-done(((bf16[2048,256]{1,0:T(8,128)(2,1)}), bf16[512,256]{1,0:T(8,128)(2,1)}) %reduce-scatter.20.cloned.1.call-update) | async-done | bytes 262160 | tf_op jit(solution)/shard_map/reduce_scatter | solution.py:223
  1059.6 57.1 %reduce-scatter.18.cloned.1.call-done = bf16[160,2048]{1,0:T(8,128)(2,1)} async-done(((bf16[1280,2048]{1,0:T(8,128)(2,1)}), bf16[160,2048]{1,0:T(8,128)(2,1)}) %reduce-scatter.18.cloned.1.call-update) | async-done | bytes 655376 | tf_op jit(solution)/shard_map/reduce_scatter | solution.py:216
  1118.3 39.8 %all-reduce = (f32[2048]{0:T(1024)}, f32[2048]{0:T(1024)}) all-reduce(f32[2048]{0:T(1024)S(1)} %get-tuple-element.54, f32[2048]{0:T(1024)S(1)} %get-tuple-element.52), channel_id=1, replica_groups=mesh['fsdp'=4,'tensor'=8] {'fsdp','tensor'}, use_global_device_ids=true, to_apply=%region_14.15 | all-reduce | flops 4096 | bytes 32768 | tf_op jit(solution)/shard_map/psum | solution.py:221
  1158.0 19.3 %reduce-scatter.14.cloned.1.call-done = bf16[160,2048]{1,0:T(8,128)(2,1)} async-done(((bf16[1280,2048]{1,0:T(8,128)(2,1)}), bf16[160,2048]{1,0:T(8,128)(2,1)}) %reduce-scatter.14.cloned.1.call-update) | async-done | bytes 655376 | tf_op jit(solution)/shard_map/reduce_scatter | solution.py:164
  (208 shorter events, 226.5 us)
Async XLA Ops:
  7.2 33.1 %all-gather.17.cloned.1.call-start = ((), (), s32[]{:S(2)}) async-start(), calls=%async_computation.14 | async-start | bytes 1310720 | tf_op jit(solution)/shard_map/all_gather | solution.py:122
  7.9 75.4 %all-gather.11.cloned.1.call-start = ((), (), s32[]{:S(2)}) async-start(), calls=%async_computation.11 | async-start | bytes 5898240 | tf_op jit(solution)/shard_map/all_gather | solution.py:141
  12.7 100.2 %all-gather.15.cloned.1.call-start = ((), (), s32[]{:S(2)}) async-start(), calls=%async_computation.13 | async-start | bytes 1310720 | tf_op jit(solution)/shard_map/all_gather | solution.py:121
  13.4 128.3 %all-gather.13.cloned.1.call-start = ((), (), s32[]{:S(2)}) async-start(), calls=%async_computation.12 | async-start | bytes 1310720 | tf_op jit(solution)/shard_map/all_gather | solution.py:123
  14.0 156.6 %all-gather.19.cloned.1.call-start = ((), (), s32[]{:S(2)}) async-start(), calls=%async_computation.15 | async-start | bytes 1310720 | tf_op jit(solution)/shard_map/all_gather | solution.py:124
  14.6 244.0 %reduce-scatter.12.cloned.1.call-start = ((), (), s32[]{:S(2)}) async-start(), calls=%async_computation.16 | async-start | bytes 11796480 | tf_op jit(solution)/shard_map/reduce_scatter | solution.py:151
  177.4 185.3 %all-gather.25.cloned.1.call-start = ((), (), s32[]{:S(2)}) async-start(), calls=%async_computation.19 | async-start | bytes 5242880 | tf_op jit(solution)/shard_map/all_gather | solution.py:126
  178.1 204.9 %all-gather.21.cloned.1.call-start = ((), (), s32[]{:S(2)}) async-start(), calls=%async_computation.17 | async-start | bytes 5898240 | tf_op jit(solution)/shard_map/all_gather | solution.py:158
  261.2 204.2 %all-gather.23.cloned.1.call-start = ((), (), s32[]{:S(2)}) async-start(), calls=%async_computation.18 | async-start | bytes 5242880 | tf_op jit(solution)/shard_map/all_gather | solution.py:125
  261.9 284.2 %all-gather.27.cloned.1.call-start = ((), (), s32[]{:S(2)}) async-start(), calls=%async_computation.20 | async-start | bytes 5242880 | tf_op jit(solution)/shard_map/all_gather | solution.py:127
  262.0 11.0 collective-permute-start
  273.0 10.9 collective-permute-start.1
  283.9 10.9 collective-permute-start.2
  295.6 10.9 collective-permute-start.3
  307.4 10.9 collective-permute-start.4
  319.1 11.0 collective-permute-start.5
  330.1 11.2 collective-permute-start.6
  330.2 329.9 %reduce-scatter.16.cloned.1.call-start = ((), (), s32[]{:S(2)}) async-start(), calls=%async_computation.22 | async-start | bytes 11796480 | tf_op jit(solution)/shard_map/reduce_scatter | solution.py:193
  579.8 125.8 %all-gather.29.cloned.1.call-start = ((), (), s32[]{:S(2)}) async-start(), calls=%async_computation.23 | async-start | bytes 5898240 | tf_op jit(solution)/shard_map/all_gather | solution.py:199
  664.4 157.6 %reduce-scatter.32.cloned.1.call-start = ((), (), s32[]{:S(2)}) async-start(), calls=%async_computation.31 | async-start | bytes 5242880 | tf_op jit(solution)/shard_map/reduce_scatter | solution.py:241
  674.4 189.9 %reduce-scatter.30.cloned.1.call-start = ((), (), s32[]{:S(2)}) async-start(), calls=%async_computation.30 | async-start | bytes 5242880 | tf_op jit(solution)/shard_map/reduce_scatter | solution.py:238
  684.7 259.1 %reduce-scatter.28.cloned.1.call-start = ((), (), s32[]{:S(2)}) async-start(), calls=%async_computation.29 | async-start | bytes 5242880 | tf_op jit(solution)/shard_map/reduce_scatter | solution.py:235
  695.0 278.7 %reduce-scatter.26.cloned.1.call-start = ((), (), s32[]{:S(2)}) async-start(), calls=%async_computation.28 | async-start | bytes 1310720 | tf_op jit(solution)/shard_map/reduce_scatter | solution.py:232
  710.7 291.0 %reduce-scatter.24.cloned.1.call-start = ((), (), s32[]{:S(2)}) async-start(), calls=%async_computation.27 | async-start | bytes 1310720 | tf_op jit(solution)/shard_map/reduce_scatter | solution.py:229
  747.5 282.3 %reduce-scatter.22.cloned.1.call-start = ((), (), s32[]{:S(2)}) async-start(), calls=%async_computation.26 | async-start | bytes 1310720 | tf_op jit(solution)/shard_map/reduce_scatter | solution.py:226
  789.6 268.3 %reduce-scatter.20.cloned.1.call-start = ((), (), s32[]{:S(2)}) async-start(), calls=%async_computation.25 | async-start | bytes 1310720 | tf_op jit(solution)/shard_map/reduce_scatter | solution.py:223
  794.8 322.0 %reduce-scatter.18.cloned.1.call-start = ((), (), s32[]{:S(2)}) async-start(), calls=%async_computation.24 | async-start | bytes 5898240 | tf_op jit(solution)/shard_map/reduce_scatter | solution.py:216
  812.0 365.3 %reduce-scatter.14.cloned.1.call-start = ((), (), s32[]{:S(2)}) async-start(), calls=%async_computation.21 | async-start | bytes 5898240 | tf_op jit(solution)/shard_map/reduce_scatter | solution.py:164
  824.9 291.8 %copy-start.1 = (bf16[160,2048]{1,0:T(8,128)(2,1)S(1)}, bf16[160,2048]{1,0:T(8,128)(2,1)}, u32[]{:S(2)}) copy-start(bf16[160,2048]{1,0:T(8,128)(2,1)} %param.12) | copy-start | bytes 1966084
  824.9 291.8 %copy-start.29 = (f32[2048]{0:T(1024)S(1)}, f32[2048]{0:T(1024)}, u32[]{:S(2)}) copy-start(f32[2048]{0:T(1024)} %copy-done.28) | copy-start | bytes 24580
  824.9 291.8 %copy-start.31 = (f32[160]{0:T(256)S(1)}, f32[160]{0:T(256)}, u32[]{:S(2)}) copy-start(f32[160]{0:T(256)} %copy-done.30) | copy-start | bytes 1924
  824.9 352.4 %copy-start.2 = (f32[160,2048]{1,0:T(8,128)S(1)}, f32[160,2048]{1,0:T(8,128)}, u32[]{:S(2)}) copy-start(f32[160,2048]{1,0:T(8,128)} %reduce-scatter.16.cloned.1.call-done) | copy-start | bytes 3932164
  (35 other events, 554.0 us)
Sparse Core Ops, SparseCore 0:
  9.6 30.6 all-gather.16
  42.8 40.5 all-gather.10
  84.9 27.9 all-gather.14
  114.3 27.4 all-gather.12
  143.2 27.4 all-gather.18
  177.5 81.0 reduce-scatter.11
  260.1 80.7 all-gather.24
  343.4 39.6 all-gather.20
  384.6 80.7 all-gather.22
  466.8 79.2 all-gather.26
  580.0 80.0 reduce-scatter.15
  664.6 41.0 all-gather.28
  708.0 76.7 reduce-scatter.31
  787.0 77.2 reduce-scatter.29
  866.5 77.2 reduce-scatter.27
  946.0 27.6 reduce-scatter.25
  975.8 25.7 reduce-scatter.23
  1003.9 25.7 reduce-scatter.21
  1032.0 25.7 reduce-scatter.19
  1061.5 55.2 reduce-scatter.17
  1120.1 57.1 reduce-scatter.13
